TPU v7x, 256 devices: a whole 4x4x8 slice. The times are simulated.
256 devices in a mesh: ctx: 128 (over z, x, y_lo, core), head: 2 (over y_hi).
Axes of the slice: x: 4, y: 4 (y_hi: 2, y_lo: 2; y = y_hi * 2 + y_lo), z: 8, core: 2. Of those that a mesh axis runs over, the one named last changes fastest.
Arguments:
- queries: bfloat16 [16384, 2048], P('ctx', 'head'), may hold values from -12 to 12
- barred_key_rows: bfloat16 [16384, 512], P('ctx', 'head'), may hold values from -5.5 to 5.5
- barred_value_rows: bfloat16 [16384, 512], P('ctx', 'head'), may hold values from -12 to 12
- doc_start: int32 [16384], P('ctx'), may hold values from 0 to 16383, as said below
- out_weight: bfloat16 [2048, 4096], P('head'), may hold values from -0.5 to 0.5
Outputs:
- mixed: bfloat16 [16384, 4096], P('ctx', 'head')
Inputs may be any that keep to these rules, and one draw needn't show every extreme that they name: Documents are runs of consecutive positions starting at position 0; the first has exactly 8192 tokens, each other has 2048 to 8192 tokens except the last two: the final position 16383 is a document of one token, and the one before it may be shorter; doc_start of a row is the first position of its document, so it is at most pos of that row.
All inputs are finite; a program needn't handle non-finite values.
Results may differ from a plain program's by a relative error of at most 0.015.
Values may be sent and summed in bfloat16 or wider, within the bound.
A program may use at most 128 MiB of HBM per device.

v0:
```python
import math

import jax
import jax.numpy as jnp
from jax import lax
from jax.sharding import PartitionSpec as P

HEAD_SIZE = 128
STRIPE = 64


MASKED_SCORE = -1e30


def positions(row_index, tok_dev, cycle_size):
    shard_index = row_index // tok_dev
    within = row_index % tok_dev
    return (within // STRIPE * cycle_size + shard_index) * STRIPE + within % STRIPE


def attend(state, query_block, key_block, value_block, query_pos, query_doc, key_pos, score_scale):
    running_max, running_sum, weighted = state
    scores = (
        jnp.einsum("tkgd,nkd->kgtn", query_block, key_block, preferred_element_type=jnp.float32)
        * score_scale
    )
    visible = (query_doc[:, None] <= key_pos[None, :]) & (key_pos[None, :] <= query_pos[:, None])
    scores = jnp.where(visible, scores, MASKED_SCORE)
    new_max = jnp.maximum(running_max, jnp.max(scores, axis=-1))
    weights = jnp.where(visible, jnp.exp(scores - new_max[..., None]), 0.0).astype(jnp.bfloat16)
    shrink = jnp.exp(running_max - new_max)
    running_sum = running_sum * shrink + jnp.sum(weights.astype(jnp.float32), axis=-1)
    weighted = weighted * shrink[..., None] + jnp.einsum(
        "kgtn,nkd->kgtd", weights, value_block, preferred_element_type=jnp.float32
    )
    return (new_max, running_sum, weighted)


def local(queries, barred_key_rows, barred_value_rows, doc_start, out_weight):
    tok_dev = queries.shape[0]
    key_heads = barred_key_rows.shape[1] // HEAD_SIZE
    heads_per_group = queries.shape[1] // barred_key_rows.shape[1]
    cycle_size = lax.axis_size("ctx")
    score_scale = 1.0 / math.sqrt(HEAD_SIZE)
    own_rows = lax.axis_index("ctx") * tok_dev + jnp.arange(tok_dev, dtype=jnp.int32)
    query_pos = positions(own_rows, tok_dev, cycle_size)
    query_split = queries.reshape(tok_dev, key_heads, heads_per_group, HEAD_SIZE)
    start_state = (
        jnp.full((key_heads, heads_per_group, tok_dev), MASKED_SCORE, jnp.float32),
        jnp.zeros((key_heads, heads_per_group, tok_dev), jnp.float32),
        jnp.zeros((key_heads, heads_per_group, tok_dev, HEAD_SIZE), jnp.float32),
    )
    state = start_state
    key_piece = lax.all_gather(barred_key_rows, "ctx", axis=0, tiled=True)
    value_piece = lax.all_gather(barred_value_rows, "ctx", axis=0, tiled=True)
    fetched_rows = key_piece.shape[0]
    shards = fetched_rows // tok_dev
    per_block = 4
    block_count = shards // per_block
    row_index = jnp.arange(fetched_rows, dtype=jnp.int32)
    key_pos_all = positions(row_index, tok_dev, cycle_size)
    key_blocks = key_piece.reshape(block_count, per_block * tok_dev, key_heads, HEAD_SIZE)
    value_blocks = value_piece.reshape(block_count, per_block * tok_dev, key_heads, HEAD_SIZE)
    pos_blocks = key_pos_all.reshape(block_count, per_block * tok_dev)

    def one_block(carried, block_data):
        key_block, value_block, pos_block = block_data
        return (
            attend(
                carried,
                query_split,
                key_block,
                value_block,
                query_pos,
                doc_start,
                pos_block,
                score_scale,
            ),
            None,
        )

    state, unused = lax.scan(one_block, state, (key_blocks, value_blocks, pos_blocks))
    running_max, running_sum, weighted = state
    scaled = weighted / running_sum[..., None]
    attn = (
        jnp.transpose(scaled, (2, 0, 1, 3))
        .reshape(tok_dev, key_heads * heads_per_group * HEAD_SIZE)
        .astype(jnp.bfloat16)
    )
    partial_out = jnp.dot(attn, out_weight, preferred_element_type=jnp.float32)
    return lax.psum_scatter(
        partial_out.astype(jnp.bfloat16), "head", scatter_dimension=1, tiled=True
    )


def solution(mesh):
    placed = (P("ctx", "head"), P("ctx", "head"), P("ctx", "head"), P("ctx"), P("head", None))
    return jax.shard_map(
        local, mesh=mesh, in_specs=placed, out_specs=P("ctx", "head"), check_vma=False
    )
```

profile of v0, /device:TPU:225, one launch (start us, length us, event | category | flops | bytes accessed | tf_op | source)
XLA Modules:
  0.0 617.7 jit_solution(1597774503833811170)
XLA Ops:
  9.5 219.6 %all-gather.3.cloned.1.call-done = bf16[16384,256]{1,0:T(8,128)(2,1)} async-done(((bf16[128,256]{1,0:T(8,128)(2,1)}), bf16[16384,256]{1,0:T(8,128)(2,1)}) %all-gather.3.cloned.1.call-update) | async-done | bytes 8388624 | tf_op jit(solution)/shard_map/all_gather | solution.py:54
  229.2 12.5 %reshape.30 = bf16[32,512,2,128]{3,2,1,0:T(2,128)(2,1)} reshape(bf16[16384,256]{1,0:T(8,128)(2,1)} %all-gather.3.cloned.1.call-done) | data formatting | bytes 16777216 | tf_op jit(solution)/shard_map/reshape | solution.py:62
  241.7 208.7 %all-gather.5.cloned.1.call-done = bf16[16384,256]{1,0:T(8,128)(2,1)} async-done(((bf16[128,256]{1,0:T(8,128)(2,1)}), bf16[16384,256]{1,0:T(8,128)(2,1)}) %all-gather.5.cloned.1.call-update) | async-done | bytes 8388624 | tf_op jit(solution)/shard_map/all_gather | solution.py:55
  450.4 12.5 %reshape.31 = bf16[32,512,2,128]{3,2,1,0:T(2,128)(2,1)} reshape(bf16[16384,256]{1,0:T(8,128)(2,1)} %all-gather.5.cloned.1.call-done) | data formatting | bytes 16777216 | tf_op jit(solution)/shard_map/reshape | solution.py:63
  462.9 115.4 %while.15 = (s32[]{:T(128)}, f32[2,4,128]{2,1,0:T(4,128)S(1)}, f32[2,4,128]{2,1,0:T(4,128)S(1)}, f32[2,4,128,128]{3,2,1,0:T(8,128)S(1)}, s32[128]{0:T(128)S(1)},...) while((s32[]{:T(128)}, f32[2,4,128]{2,1,0:T(4,128)S(1)}, ...), condition=%wide.region_3.4_spmd.clone, body=%wide.region_0.3_spmd.clone.sunk | while | flops 276900224 | bytes 9510541 | solution.py:82
  463.1 1.4 constant_dynamic-slice_fusion.6
  466.7 1.4 constant_dynamic-slice_fusion.6
  470.3 1.4 constant_dynamic-slice_fusion.6
  473.9 1.4 constant_dynamic-slice_fusion.6
  477.5 1.4 constant_dynamic-slice_fusion.6
  481.1 1.4 constant_dynamic-slice_fusion.6
  484.7 1.4 constant_dynamic-slice_fusion.6
  488.3 1.4 constant_dynamic-slice_fusion.6
  491.9 1.4 constant_dynamic-slice_fusion.6
  495.5 1.4 constant_dynamic-slice_fusion.6
  499.1 1.4 constant_dynamic-slice_fusion.6
  502.8 1.4 constant_dynamic-slice_fusion.6
  506.4 1.4 constant_dynamic-slice_fusion.6
  510.0 1.4 constant_dynamic-slice_fusion.6
  513.6 1.4 constant_dynamic-slice_fusion.6
  517.2 1.4 constant_dynamic-slice_fusion.6
  520.8 1.4 constant_dynamic-slice_fusion.6
  524.4 1.4 constant_dynamic-slice_fusion.6
  528.0 1.4 constant_dynamic-slice_fusion.6
  531.6 1.4 constant_dynamic-slice_fusion.6
  535.2 1.4 constant_dynamic-slice_fusion.6
  542.4 1.4 constant_dynamic-slice_fusion.6
  560.5 1.4 constant_dynamic-slice_fusion.6
  564.1 1.4 constant_dynamic-slice_fusion.6
  567.7 1.4 constant_dynamic-slice_fusion.6
  578.6 5.7 convolution_convert_fusion
  584.2 26.9 %reduce-scatter.2.cloned.1.call-done = bf16[128,2048]{1,0:T(8,128)(2,1)} async-done(((bf16[128,4096]{1,0:T(8,128)(2,1)}), bf16[128,2048]{1,0:T(8,128)(2,1)}) %reduce-scatter.2.cloned.1.call-update) | async-done | bytes 524304 | tf_op jit(solution)/shard_map/reduce_scatter | solution.py:91
  (311 shorter events, 81.6 us)
Async XLA Ops:
  6.5 222.6 %all-gather.3.cloned.1.call-start = ((), (), s32[]{:S(2)}) async-start(), calls=%async_computation.1 | async-start | bytes 8454144 | tf_op jit(solution)/shard_map/all_gather | solution.py:54
  7.3 443.1 %all-gather.5.cloned.1.call-start = ((), (), s32[]{:S(2)}) async-start(), calls=%async_computation.2 | async-start | bytes 8454144 | tf_op jit(solution)/shard_map/all_gather | solution.py:55
  8.0 603.2 %reduce-scatter.2.cloned.1.call-start = ((), (), s32[]{:S(2)}) async-start(), calls=%async_computation.3 | async-start | bytes 1572864 | tf_op jit(solution)/shard_map/reduce_scatter | solution.py:91
  241.7 221.2 %copy-start = (s32[128]{0:T(128)S(1)}, s32[128]{0:T(128)}, u32[]{:S(2)}) copy-start(s32[128]{0:T(128)} %param.10) | copy-start | bytes 1540
Sparse Core Ops, SparseCore 0:
  9.2 219.8 all-gather.2
  231.0 219.2 all-gather.4
  584.4 26.7 reduce-scatter.1
where the time goes:
time: 622 us; the launch traced here: 618 us
  waiting for transfers between devices  457 us (73%)
  local copies, waits for them, and re-layouts  71.7 us (12%)
  matrix products  51.2 us (8%)
  other arithmetic  22.9 us (4%)
  between operations  13.2 us (2%)
    all_gather x1, waiting for transfers between devices, local(): key_piece = lax.all_gather(barred_key_rows, 'ctx', axis=0, tiled=True)  220 us
    all_gather x1, waiting for transfers between devices, local(): value_piece = lax.all_gather(barred_value_rows, 'ctx', axis=0, tiled=True)  209 us
    dynamic_slice x64, local copies, waits for them, and re-layouts, local(): lax.scan(one_block, state, (key_blocks, value_blocks, pos_blocks))  45 us
    dot_general x32, matrix products, attend(): jnp.einsum('kgtn,nkd->kgtd', weights, value_block, preferred_element_type...  30.7 us
    reduce_scatter x1, waiting for transfers between devices, local(): lax.psum_scatter(partial_out.astype(jnp.bfloat16), 'head', scatter_dimens...  26.9 us
    reduce_sum x32, other arithmetic, attend(): jnp.sum(weights.astype(jnp.float32), axis=-1)  16.7 us
    dot_general x32, matrix products, attend(): jnp.einsum('tkgd,nkd->kgtn', query_block, key_block, preferred_element_ty...  14.9 us
    reshape x1, local copies, waits for them, and re-layouts, local(): key_piece.reshape(block_count, per_block * tok_dev, key_heads, HEAD_SIZE)  12.5 us
  transfers between devices with their start and end apart: 3, of which 3 were waited for; matrix products, arithmetic and copies ran while one was open for 2% of the time, Pallas kernels for 0%

commit v1 on v0

v1 whole, which is shorter than its diff:
```python
import math

import jax
import jax.numpy as jnp
from jax import lax
from jax.experimental import pallas as pl
from jax.experimental.pallas import tpu as pltpu
from jax.sharding import PartitionSpec as P

NZ, NX, NY, NC = 8, 4, 2, 2
STRIPE = 64
HEAD = 128
GROUP = 4
PLANE = NX * NY * NC * STRIPE
ROWS = GROUP * STRIPE
ROUND = NZ * PLANE
COLS = 2048
CHUNK = 256
NCH = COLS // CHUNK
MASKED = -1e30
LOG2 = math.log2(math.e) / math.sqrt(HEAD)
MESH = pl.DeviceIdType.MESH
F32 = jnp.float32
BF16 = jnp.bfloat16


def kernel(q_hbm, k_hbm, v_hbm, doc_hbm, w_hbm, out_ref,
           kv, q_in, doc_in, q_rows, doc_rows, top, acc, attn_send, attn_in, attn, w_own, part_send,
           relay, part_in, own_part,
           loc_sem, w_sem, kx_s, kx_r, qx_s, qx_r, dx_s, dx_r, z_s, z_r, c0_s, c0_r, c_s, c_r, y0_s, y0_r,
           y_s, y_r, o_s, o_r, p_s, p_r, f_s, f_r):
    c = lax.axis_index("ctx")
    h = lax.axis_index("head")
    z, x, y, core = c // 16, (c // 4) % NX, (c // 2) % NY, c % NC
    rnd = x // 2

    def dev(z_, x_, y_, k_, h_):
        return (((z_ * NX + x_) * NY + y_) * NC + k_, h_)

    up = dev((z + 1) % NZ, x, y, core, h)
    down = dev((z + NZ - 1) % NZ, x, y, core, h)
    across = dev(z, x, 1 - y, core, h)
    twin = dev(z, x, y, 1 - core, h)
    outer = dev(z, x, 1 - y, core, 1 - h)
    xs = [(x + d) % NX for d in (2, 1, 3)]

    def send(src, dst, ss, rs, to):
        cp = pltpu.make_async_remote_copy(src, dst, ss, rs, device_id=to, device_id_type=MESH)
        cp.start()

    def got(ref, ss, rs):
        pltpu.make_async_remote_copy(ref, ref, ss, rs, device_id=twin, device_id_type=MESH).wait_recv()

    def sent(ref, ss, rs):
        pltpu.make_async_remote_copy(ref, ref, ss, rs, device_id=twin, device_id_type=MESH).wait_send()

    barrier = pltpu.get_barrier_semaphore()
    peers = [up, down, across, twin, outer] + [dev(z, x_, y, core, h) for x_ in xs]
    for peer in peers:
        pl.semaphore_signal(barrier, inc=1, device_id=peer, device_id_type=MESH)

    def kv_src(ref, x_):
        return ref.at[pl.ds(pl.multiple_of(x_ // 2 * STRIPE, STRIPE), STRIPE),
                      pl.ds(pl.multiple_of(x_ % 2 * HEAD, HEAD), HEAD)]

    def q_src(x_):
        return q_hbm.at[pl.ds(pl.multiple_of(x_ // 2 * STRIPE, STRIPE), STRIPE),
                        pl.ds(pl.multiple_of(x_ % 2 * GROUP * HEAD, HEAD), GROUP * HEAD)]

    def doc_src(x_):
        return doc_hbm.at[pl.ds(pl.multiple_of(x_ // 2 * STRIPE, STRIPE), STRIPE)]

    own_copies = [
        pltpu.make_async_copy(kv_src(k_hbm, x), kv.at[z, x, y, core, 0], loc_sem.at[0]),
        pltpu.make_async_copy(kv_src(v_hbm, x), kv.at[z, x, y, core, 1], loc_sem.at[1]),
        pltpu.make_async_copy(q_src(x), q_in.at[x], loc_sem.at[2]),
        pltpu.make_async_copy(doc_src(x), doc_in.at[x], loc_sem.at[3]),
    ]
    for cp in own_copies:
        cp.start()
    pl.semaphore_wait(barrier, len(peers))

    for x_ in xs:
        to = dev(z, x_, y, core, h)
        send(kv_src(k_hbm, x_), kv.at[z, x, y, core, 0], kx_s.at[x_, 0], kx_r.at[x, 0], to)
        send(kv_src(v_hbm, x_), kv.at[z, x, y, core, 1], kx_s.at[x_, 1], kx_r.at[x, 1], to)
    for x_ in xs:
        to = dev(z, x_, y, core, h)
        send(q_src(x_), q_in.at[x], qx_s.at[x_], qx_r.at[x], to)
        send(doc_src(x_), doc_in.at[x], dx_s.at[x_], dx_r.at[x], to)

    w_copies = [
        pltpu.make_async_copy(w_hbm.at[:, pl.ds(pl.multiple_of((1 - h) * COLS, COLS), COLS)], w_own.at[0], w_sem.at[0]),
        pltpu.make_async_copy(w_hbm.at[:, pl.ds(pl.multiple_of(h * COLS, COLS), COLS)], w_own.at[1], w_sem.at[1]),
    ]

    def part_ref(zp, part, half=None):
        xb = 2 * (((part + 1) // 2 + 1) % 2)
        yy = (y + part // 2) % 2
        if half is None:
            return kv.at[zp, pl.ds(xb, 2), yy, core]
        return kv.at[zp, pl.ds(xb + half, 1), yy, core]

    own_copies[0].wait()
    own_copies[1].wait()
    for x_ in xs:
        got(kv.at[z, x_, y, core, 0], kx_s.at[x_, 0], kx_r.at[x_, 0])
        got(kv.at[z, x_, y, core, 1], kx_s.at[x_, 1], kx_r.at[x_, 1])
    for part in (1, 0):
        ref = part_ref(z, part)
        send(ref, ref, y0_s.at[part], y0_r.at[part], across)
        send(ref, ref, z_s.at[0, 0, part], z_r.at[0, 0, part], up)
        send(ref, ref, z_s.at[1, 0, part], z_r.at[1, 0, part], down)
        send(ref, ref, c0_s.at[part], c0_r.at[part], twin)
    for cp in w_copies:
        cp.start()
    ref = part_ref(z, 2)
    got(ref, y0_s.at[1], y0_r.at[1])
    send(ref, ref, z_s.at[0, 0, 2], z_r.at[0, 0, 2], up)
    send(ref, ref, z_s.at[1, 0, 2], z_r.at[1, 0, 2], down)
    send(ref, ref, c0_s.at[2], c0_r.at[2], twin)
    ref = part_ref(z, 3)
    got(ref, y0_s.at[0], y0_r.at[0])
    send(ref, ref, c0_s.at[3], c0_r.at[3], twin)

    def twin_ref(zp, part, half=None):
        xb = 2 * (((part + 1) // 2 + 1) % 2)
        yy = (y + part // 2) % 2
        if half is None:
            return kv.at[zp, pl.ds(xb, 2), yy, 1 - core]
        return kv.at[zp, pl.ds(xb + half, 1), yy, 1 - core]

    def work(plane, rb, own, docs):
        keys = kv[plane, :, :, :, 0].reshape(PLANE, HEAD)
        values = kv[plane, :, :, :, 1].reshape(PLANE, HEAD)
        s = lax.dot_general(q_rows[rb], keys, (((1,), (1,)), ((), ())), preferred_element_type=F32)
        if docs:
            kpos = rnd * ROUND + plane * PLANE + lax.broadcasted_iota(jnp.int32, (ROWS, PLANE), 1)
            seen = kpos >= jnp.tile(doc_rows[rb], (1, PLANE // HEAD))
            if own:
                first = rnd * ROUND + (z * 16 + rb * 4 + y * 2 + core) * STRIPE
                qpos = first + lax.broadcasted_iota(jnp.int32, (ROWS, PLANE), 0) % STRIPE
                seen = seen & (kpos <= qpos)
            s = jnp.where(seen, s, MASKED)
        old = top[rb]
        new = jnp.maximum(old, jnp.max(s, axis=1, keepdims=True))
        p = jnp.exp2(s * LOG2 - jnp.tile(new * LOG2, (1, PLANE // HEAD))).astype(BF16)
        shrink = jnp.exp2((old - new) * LOG2)
        both = jnp.concatenate([values, jnp.ones((PLANE, HEAD), BF16)], axis=1)
        acc[rb] = acc[rb] * jnp.tile(shrink, (1, 2)) + jnp.dot(p, both, preferred_element_type=F32)
        top[rb] = new

    def chunk(d, side, rb):
        plane = (z + NZ - d + 2 * d * side) % NZ
        earlier = (d > 0) & (plane < z)

        @pl.when((d == 0) & (side == 0))
        def _():
            work(z, rb, True, True)

        @pl.when(earlier & (rnd == 1))
        def _():
            work(plane, rb, False, True)

        @pl.when(earlier & (rnd == 0))
        def _():
            work(plane, rb, False, False)

    def event(t, carry):
        s = t // 8 + 1
        e = t % 8
        side, part = e % 2, e // 2
        plane = (z + NZ - s + 2 * s * side) % NZ
        nxt = dev((z + 1 + (NZ - 2) * side) % NZ, x, y, core, h)

        @pl.when((s <= 3) & (part <= 2))
        def _():
            got(part_ref(plane, part), z_s.at[side, s - 1, part], z_r.at[side, s - 1, part])

        @pl.when((s == 4) & (part <= 2))
        def _():
            got(part_ref(plane, part, side), z_s.at[side, 3, part], z_r.at[side, 3, part])

        @pl.when((s <= 3) & (part == 3))
        def _():
            got(part_ref(plane, 3), y_s.at[s - 1, side], y_r.at[s - 1, side])

        @pl.when((s == 4) & (part == 3))
        def _():
            got(part_ref(plane, 3, side), y_s.at[3, side], y_r.at[3, side])

        @pl.when((s <= 2) & (part <= 2))
        def _():
            r = part_ref(plane, part)
            send(r, r, z_s.at[side, s, part], z_r.at[side, s, part], nxt)

        @pl.when((s == 3) & (part <= 2))
        def _():
            r = part_ref(plane, part, side)
            send(r, r, z_s.at[side, 3, part], z_r.at[side, 3, part], nxt)

        @pl.when(s <= 3)
        def _():
            r = part_ref(plane, part)

            @pl.when(part == 0)
            def _():
                send(r, r, y_s.at[s - 1, side], y_r.at[s - 1, side], across)

            send(r, r, c_s.at[s - 1, side, part], c_r.at[s - 1, side, part], twin)

        @pl.when(s == 4)
        def _():
            r = part_ref(plane, part, side)

            @pl.when(part == 0)
            def _():
                send(r, r, y_s.at[3, side], y_r.at[3, side], across)

            send(r, r, c_s.at[3, side, part], c_r.at[3, side, part], twin)

        @pl.when(t == 0)
        def _():
            own_copies[2].wait()
            own_copies[3].wait()
            for x_ in xs:
                got(q_in.at[x_], qx_s.at[x_], qx_r.at[x_])
                got(doc_in.at[x_], dx_s.at[x_], dx_r.at[x_])
            for part_ in range(4):
                got(twin_ref(z, part_), c0_s.at[part_], c0_r.at[part_])
            for rb_ in range(NX):
                for g in range(GROUP):
                    q_rows[rb_, g * STRIPE:(g + 1) * STRIPE] = q_in[rb_, :, g * HEAD:(g + 1) * HEAD]
                    doc_rows[rb_, g * STRIPE:(g + 1) * STRIPE] = doc_in[rb_]
            top[...] = jnp.full(top.shape, MASKED, F32)
            acc[...] = jnp.zeros(acc.shape, F32)

        cs, rb = e // 4, e % 4

        @pl.when((s > 1) & (rb == 0))
        def _():
            back = (z + NZ - (s - 1) + 2 * (s - 1) * cs) % NZ
            for part_ in range(4):
                got(twin_ref(back, part_), c_s.at[s - 2, cs, part_], c_r.at[s - 2, cs, part_])

        chunk(s - 1, cs, rb)
        return carry

    lax.fori_loop(0, 32, event, 0)

    far = (z + 4) % NZ
    for side in range(2):
        for part in range(4):
            got(twin_ref(far, part, side), c_s.at[3, side, part], c_r.at[3, side, part])

    def last(rb, carry):
        chunk(4, 0, rb)
        total = acc[rb]
        o = (total[:, :HEAD] / total[:, HEAD:]).astype(BF16)
        for g in range(GROUP):
            attn_send[rb, :, g * HEAD:(g + 1) * HEAD] = o[g * STRIPE:(g + 1) * STRIPE]

        @pl.when(rb != x)
        def _():
            send(attn_send.at[rb], attn_in.at[x], o_s.at[rb], o_r.at[x], dev(z, rb, y, core, h))

        return carry

    lax.fori_loop(0, NX, last, 0)
    attn_in[x] = attn_send[x]

    for cp in w_copies:
        cp.wait()
    for x_ in xs:
        got(attn_in.at[x_], o_s.at[x_], o_r.at[x_])
    for kind in range(NX):
        attn[kind // 2 * STRIPE:(kind // 2 + 1) * STRIPE,
             kind % 2 * GROUP * HEAD:(kind % 2 + 1) * GROUP * HEAD] = attn_in[kind]

    for j in range(NCH):
        piece = jnp.dot(attn[...], w_own[0, :, j * CHUNK:(j + 1) * CHUNK], preferred_element_type=F32)
        part_send[j] = piece.astype(BF16)
        way, i = j % 2, j // 2
        send(part_send.at[j], relay.at[way, i], p_s.at[way, i], p_r.at[way, i], across if way == 0 else outer)
    for i in range(NCH // 2):
        for way in range(2):
            got(relay.at[way, i], p_s.at[way, i], p_r.at[way, i])
            send(relay.at[way, i], part_in.at[2 * i + way], f_s.at[way, i], f_r.at[way, i],
                 outer if way == 0 else across)
        for j in (2 * i, 2 * i + 1):
            own_part[:, j * CHUNK:(j + 1) * CHUNK] = jnp.dot(
                attn[...], w_own[1, :, j * CHUNK:(j + 1) * CHUNK], preferred_element_type=F32)
    for j in range(NCH):
        way, i = j % 2, j // 2
        got(part_in.at[j], f_s.at[way, i], f_r.at[way, i])
        cols = slice(j * CHUNK, (j + 1) * CHUNK)
        out_ref[:, cols] = (own_part[:, cols] + part_in[j].astype(F32)).astype(BF16)

    for x_ in xs:
        for n in range(2):
            sent(kv.at[z, x_, y, core, n], kx_s.at[x_, n], kx_r.at[x_, n])
        sent(q_in.at[x_], qx_s.at[x_], qx_r.at[x_])
        sent(doc_in.at[x_], dx_s.at[x_], dx_r.at[x_])
        sent(attn_send.at[x_], o_s.at[x_], o_r.at[x_])
    for part in range(2):
        sent(part_ref(z, part), y0_s.at[part], y0_r.at[part])
    for part in range(4):
        sent(part_ref(z, part), c0_s.at[part], c0_r.at[part])
    for n in range(4):
        for side in range(2):
            half = side if n == 3 else None
            for part in range(3):
                sent(part_ref(z, part, half), z_s.at[side, n, part], z_r.at[side, n, part])
            for part in range(4):
                sent(part_ref(z, part, half), c_s.at[n, side, part], c_r.at[n, side, part])
            sent(part_ref(z, 0, half), y_s.at[n, side], y_r.at[n, side])
    for way in range(2):
        for i in range(NCH // 2):
            sent(relay.at[way, i], p_s.at[way, i], p_r.at[way, i])
            sent(relay.at[way, i], f_s.at[way, i], f_r.at[way, i])


def local(queries, keys, values, doc_start, out_weight):
    docs = jnp.broadcast_to(doc_start[:, None], (doc_start.shape[0], HEAD))
    dma = pltpu.SemaphoreType.DMA
    anyspace = pl.BlockSpec(memory_space=pl.ANY)
    return pl.pallas_call(
        kernel,
        out_shape=jax.ShapeDtypeStruct((2 * STRIPE, COLS), BF16),
        in_specs=[anyspace] * 5,
        out_specs=pl.BlockSpec(memory_space=pltpu.VMEM),
        scratch_shapes=[
            pltpu.VMEM((NZ, NX, NY, NC, 2, STRIPE, HEAD), BF16),
            pltpu.VMEM((NX, STRIPE, GROUP * HEAD), BF16),
            pltpu.VMEM((NX, STRIPE, HEAD), jnp.int32),
            pltpu.VMEM((NX, ROWS, HEAD), BF16),
            pltpu.VMEM((NX, ROWS, HEAD), jnp.int32),
            pltpu.VMEM((NX, ROWS, HEAD), F32),
            pltpu.VMEM((NX, ROWS, 2 * HEAD), F32),
            pltpu.VMEM((NX, STRIPE, GROUP * HEAD), BF16),
            pltpu.VMEM((NX, STRIPE, GROUP * HEAD), BF16),
            pltpu.VMEM((2 * STRIPE, 2 * GROUP * HEAD), BF16),
            pltpu.VMEM((2, 2 * GROUP * HEAD, COLS), BF16),
            pltpu.VMEM((NCH, 2 * STRIPE, CHUNK), BF16),
            pltpu.VMEM((2, NCH // 2, 2 * STRIPE, CHUNK), BF16),
            pltpu.VMEM((NCH, 2 * STRIPE, CHUNK), BF16),
            pltpu.VMEM((2 * STRIPE, COLS), F32),
            dma((4,)), dma((2,)),
            dma((NX, 2)), dma((NX, 2)), dma((NX,)), dma((NX,)), dma((NX,)), dma((NX,)),
            dma((2, 4, 3)), dma((2, 4, 3)), dma((4,)), dma((4,)), dma((4, 2, 4)), dma((4, 2, 4)),
            dma((2,)), dma((2,)), dma((4, 2)), dma((4, 2)), dma((NX,)), dma((NX,)),
            dma((2, NCH // 2)), dma((2, NCH // 2)), dma((2, NCH // 2)), dma((2, NCH // 2)),
        ],
        compiler_params=pltpu.CompilerParams(
            collective_id=0, has_side_effects=True, vmem_limit_bytes=56 * 1024 * 1024),
    )(queries, keys, values, docs, out_weight)


def solution(mesh):
    placed = (P("ctx", "head"), P("ctx", "head"), P("ctx", "head"), P("ctx"), P("head", None))
    return jax.shard_map(local, mesh=mesh, in_specs=placed, out_specs=P("ctx", "head"), check_vma=False)
```

time: 622 us -> 72.2 us (0.12)
  waiting for transfers between devices: 457 us -> 0 us
  local copies, waits for them, and re-layouts: 71.7 us -> 3.25 us
  Pallas kernels: 0 us -> 67.6 us
  matrix products: 51.2 us -> 0 us
  other arithmetic: 22.9 us -> 0 us
  between operations: 13.2 us -> 0.01 us
    all_gather x2 -> x0, waiting for transfers between devices: 428 us -> none  [the longest x1 220 us: local(): key_piece = lax.all_gather(barred_key_rows, 'ctx', axis=0, tiled=True)]
    pallas_call x0 -> x1, Pallas kernels: none -> 67.6 us  [local(): pl.pallas_call(kernel, out_shape=jax.ShapeDtypeStruct((2 * STRIPE, COLS),...]
    dot_general x65 -> x0, matrix products: 51.2 us -> none  [the longest x32 30.7 us: attend(): jnp.einsum('kgtn,nkd->kgtd', weights, value_block, preferred_element_type...]
    dynamic_slice x64 -> x0, local copies, waits for them, and re-layouts: 45 us -> none  [local(): lax.scan(one_block, state, (key_blocks, value_blocks, pos_blocks))]
    reduce_scatter x1 -> x0, waiting for transfers between devices: 26.9 us -> none  [local(): lax.psum_scatter(partial_out.astype(jnp.bfloat16), 'head', scatter_dimens...]
    reshape x2 -> x0, local copies, waits for them, and re-layouts: 25.1 us -> none  [the longest x1 12.5 us: local(): key_piece.reshape(block_count, per_block * tok_dev, key_heads, HEAD_SIZE)]
    reduce_sum x32 -> x0, other arithmetic: 16.7 us -> none  [attend(): jnp.sum(weights.astype(jnp.float32), axis=-1)]
  transfers between devices with their start and end apart: 3 -> 0, of which waited for: 3 -> 0; matrix products, arithmetic and copies ran while one was open for 2% -> 0% of each run, Pallas kernels for 0% -> 0%
where the time goes in v1:
time: 72.2 us; the launch traced here: 70.9 us
  Pallas kernels  67.6 us (94%)
  local copies, waits for them, and re-layouts  3.25 us (5%)
    pallas_call x1, Pallas kernels, local(): pl.pallas_call(kernel, out_shape=jax.ShapeDtypeStruct((2 * STRIPE, COLS),...  67.6 us
    unnamed x1, local copies, waits for them, and re-layouts  1.88 us

profile of v1, /device:TPU:225, one launch (start us, length us, event | category | flops | bytes accessed | tf_op | source)
XLA Modules:
  0.0 70.9 jit_solution(15613576215091839125)
XLA Ops:
  0.0 1.4 %broadcast_in_dim.2.doc_hbm = s32[128,128]{1,0:T(8,128)} broadcast(s32[128]{0:T(128)} %param.8), dimensions={0} | broadcast | bytes 66048 | tf_op jit(solution)/shard_map/broadcast_in_dim | solution.py:324
  1.4 67.6 %shard_map.55 = bf16[128,2048]{1,0:T(8,128)(2,1)} custom-call(bf16[128,1024]{1,0:T(8,128)(2,1)} %q_hbm.1, bf16[128,256]{1,0:T(8,128)(2,1)} %k_hbm.1, bf16[128,256]{1,0:T(8,128)(2,1)} %v_hbm.1, s32[128,128]{1,0:T(8,128)} %broadcast_in_dim.2.doc_hbm, bf16[1024,4096]{1,0:T(8,128)(2,1)} %w_hbm.1), custom_call_target="tpu_custom_call" | custom-call | tf_op jit(solution)/shard_map/pallas_call | solution.py:327
  69.0 1.9 %copy.7 = bf16[128,2048]{1,0:T(8,128)(2,1)} copy(bf16[128,2048]{1,0:T(8,128)(2,1)} %shard_map.55) | data formatting | bytes 1048576

commit v2 on v1

--- a/solution.py
+++ b/solution.py
@@ -13,6 +13,7 @@
 GROUP = 4
 PLANE = NX * NY * NC * STRIPE
 ROWS = GROUP * STRIPE
+BLOCK = NY * NC * STRIPE
 ROUND = NZ * PLANE
 COLS = 2048
 CHUNK = 256
@@ -26,9 +27,9 @@
 
 def kernel(q_hbm, k_hbm, v_hbm, doc_hbm, w_hbm, out_ref,
            kv, q_in, doc_in, q_rows, doc_rows, top, acc, attn_send, attn_in, attn, w_own, part_send,
-           relay, part_in, own_part,
+           part_in, own_part,
            loc_sem, w_sem, kx_s, kx_r, qx_s, qx_r, dx_s, dx_r, z_s, z_r, c0_s, c0_r, c_s, c_r, y0_s, y0_r,
-           y_s, y_r, o_s, o_r, p_s, p_r, f_s, f_r):
+           y_s, y_r, o_s, o_r, p_s, p_r):
     c = lax.axis_index("ctx")
     h = lax.axis_index("head")
     z, x, y, core = c // 16, (c // 4) % NX, (c // 2) % NY, c % NC
@@ -41,7 +42,7 @@
     down = dev((z + NZ - 1) % NZ, x, y, core, h)
     across = dev(z, x, 1 - y, core, h)
     twin = dev(z, x, y, 1 - core, h)
-    outer = dev(z, x, 1 - y, core, 1 - h)
+    partner = dev(z, x, y, core, 1 - h)
     xs = [(x + d) % NX for d in (2, 1, 3)]
 
     def send(src, dst, ss, rs, to):
@@ -55,7 +56,7 @@
         pltpu.make_async_remote_copy(ref, ref, ss, rs, device_id=twin, device_id_type=MESH).wait_send()
 
     barrier = pltpu.get_barrier_semaphore()
-    peers = [up, down, across, twin, outer] + [dev(z, x_, y, core, h) for x_ in xs]
+    peers = [up, down, across, twin, partner] + [dev(z, x_, y, core, h) for x_ in xs]
     for peer in peers:
         pl.semaphore_signal(barrier, inc=1, device_id=peer, device_id_type=MESH)
 
@@ -66,15 +67,12 @@
     def q_src(x_):
         return q_hbm.at[pl.ds(pl.multiple_of(x_ // 2 * STRIPE, STRIPE), STRIPE),
                         pl.ds(pl.multiple_of(x_ % 2 * GROUP * HEAD, HEAD), GROUP * HEAD)]
-
-    def doc_src(x_):
-        return doc_hbm.at[pl.ds(pl.multiple_of(x_ // 2 * STRIPE, STRIPE), STRIPE)]
 
     own_copies = [
         pltpu.make_async_copy(kv_src(k_hbm, x), kv.at[z, x, y, core, 0], loc_sem.at[0]),
         pltpu.make_async_copy(kv_src(v_hbm, x), kv.at[z, x, y, core, 1], loc_sem.at[1]),
         pltpu.make_async_copy(q_src(x), q_in.at[x], loc_sem.at[2]),
-        pltpu.make_async_copy(doc_src(x), doc_in.at[x], loc_sem.at[3]),
+        pltpu.make_async_copy(doc_hbm, doc_in.at[x], loc_sem.at[3]),
     ]
     for cp in own_copies:
         cp.start()
@@ -87,7 +85,7 @@
     for x_ in xs:
         to = dev(z, x_, y, core, h)
         send(q_src(x_), q_in.at[x], qx_s.at[x_], qx_r.at[x], to)
-        send(doc_src(x_), doc_in.at[x], dx_s.at[x_], dx_r.at[x], to)
+        send(doc_hbm, doc_in.at[x], dx_s.at[x_], dx_r.at[x], to)
 
     w_copies = [
         pltpu.make_async_copy(w_hbm.at[:, pl.ds(pl.multiple_of((1 - h) * COLS, COLS), COLS)], w_own.at[0], w_sem.at[0]),
@@ -131,24 +129,32 @@
         return kv.at[zp, pl.ds(xb + half, 1), yy, 1 - core]
 
     def work(plane, rb, own, docs):
-        keys = kv[plane, :, :, :, 0].reshape(PLANE, HEAD)
-        values = kv[plane, :, :, :, 1].reshape(PLANE, HEAD)
-        s = lax.dot_general(q_rows[rb], keys, (((1,), (1,)), ((), ())), preferred_element_type=F32)
-        if docs:
-            kpos = rnd * ROUND + plane * PLANE + lax.broadcasted_iota(jnp.int32, (ROWS, PLANE), 1)
-            seen = kpos >= jnp.tile(doc_rows[rb], (1, PLANE // HEAD))
-            if own:
-                first = rnd * ROUND + (z * 16 + rb * 4 + y * 2 + core) * STRIPE
-                qpos = first + lax.broadcasted_iota(jnp.int32, (ROWS, PLANE), 0) % STRIPE
-                seen = seen & (kpos <= qpos)
-            s = jnp.where(seen, s, MASKED)
-        old = top[rb]
-        new = jnp.maximum(old, jnp.max(s, axis=1, keepdims=True))
-        p = jnp.exp2(s * LOG2 - jnp.tile(new * LOG2, (1, PLANE // HEAD))).astype(BF16)
-        shrink = jnp.exp2((old - new) * LOG2)
-        both = jnp.concatenate([values, jnp.ones((PLANE, HEAD), BF16)], axis=1)
-        acc[rb] = acc[rb] * jnp.tile(shrink, (1, 2)) + jnp.dot(p, both, preferred_element_type=F32)
-        top[rb] = new
+        def scores(b):
+            keys = kv[plane, b, :, :, 0].reshape(BLOCK, HEAD)
+            s = lax.dot_general(q_rows[rb], keys, (((1,), (1,)), ((), ())), preferred_element_type=F32)
+            if docs:
+                kpos = rnd * ROUND + plane * PLANE + b * BLOCK + lax.broadcasted_iota(jnp.int32, (ROWS, BLOCK), 1)
+                seen = kpos >= jnp.tile(doc_rows[rb], (1, BLOCK // HEAD))
+                if own:
+                    first = rnd * ROUND + (z * 16 + rb * 4 + y * 2 + core) * STRIPE
+                    qpos = first + lax.broadcasted_iota(jnp.int32, (ROWS, BLOCK), 0) % STRIPE
+                    seen = seen & (kpos <= qpos)
+                s = jnp.where(seen, s, MASKED)
+            return s
+
+        old, total = top[rb], acc[rb]
+        s = scores(0)
+        for b in range(NX):
+            ahead = scores(b + 1) if b + 1 < NX else None
+            new = jnp.maximum(old, jnp.max(s, axis=1, keepdims=True))
+            p = jnp.exp2(s * LOG2 - jnp.tile(new * LOG2, (1, BLOCK // HEAD))).astype(BF16)
+            shrink = jnp.exp2((old - new) * LOG2)
+            values = kv[plane, b, :, :, 1].reshape(BLOCK, HEAD)
+            both = jnp.concatenate([values, jnp.ones((BLOCK, HEAD), BF16)], axis=1)
+            total = total * jnp.tile(shrink, (1, 2)) + jnp.dot(p, both, preferred_element_type=F32)
+            old, s = new, ahead
+        acc[rb] = total
+        top[rb] = old
 
     def chunk(d, side, rb):
         plane = (z + NZ - d + 2 * d * side) % NZ
@@ -229,9 +235,12 @@
             for part_ in range(4):
                 got(twin_ref(z, part_), c0_s.at[part_], c0_r.at[part_])
             for rb_ in range(NX):
+                line = jnp.broadcast_to(doc_in[rb_].astype(F32), (HEAD, HEAD))
+                line = jnp.transpose(line).astype(jnp.int32)
+                line = jnp.where(rnd == 1, line[STRIPE:], line[:STRIPE])
                 for g in range(GROUP):
                     q_rows[rb_, g * STRIPE:(g + 1) * STRIPE] = q_in[rb_, :, g * HEAD:(g + 1) * HEAD]
-                    doc_rows[rb_, g * STRIPE:(g + 1) * STRIPE] = doc_in[rb_]
+                    doc_rows[rb_, g * STRIPE:(g + 1) * STRIPE] = line
             top[...] = jnp.full(top.shape, MASKED, F32)
             acc[...] = jnp.zeros(acc.shape, F32)
 
@@ -277,24 +286,26 @@
         attn[kind // 2 * STRIPE:(kind // 2 + 1) * STRIPE,
              kind % 2 * GROUP * HEAD:(kind % 2 + 1) * GROUP * HEAD] = attn_in[kind]
 
-    for j in range(NCH):
-        piece = jnp.dot(attn[...], w_own[0, :, j * CHUNK:(j + 1) * CHUNK], preferred_element_type=F32)
-        part_send[j] = piece.astype(BF16)
-        way, i = j % 2, j // 2
-        send(part_send.at[j], relay.at[way, i], p_s.at[way, i], p_r.at[way, i], across if way == 0 else outer)
-    for i in range(NCH // 2):
-        for way in range(2):
-            got(relay.at[way, i], p_s.at[way, i], p_r.at[way, i])
-            send(relay.at[way, i], part_in.at[2 * i + way], f_s.at[way, i], f_r.at[way, i],
-                 outer if way == 0 else across)
-        for j in (2 * i, 2 * i + 1):
-            own_part[:, j * CHUNK:(j + 1) * CHUNK] = jnp.dot(
-                attn[...], w_own[1, :, j * CHUNK:(j + 1) * CHUNK], preferred_element_type=F32)
-    for j in range(NCH):
-        way, i = j % 2, j // 2
-        got(part_in.at[j], f_s.at[way, i], f_r.at[way, i])
-        cols = slice(j * CHUNK, (j + 1) * CHUNK)
+    def theirs(j, carry):
+        cols = pl.ds(pl.multiple_of(j * CHUNK, CHUNK), CHUNK)
+        part_send[j] = jnp.dot(attn[...], w_own[0, :, cols], preferred_element_type=F32).astype(BF16)
+        send(part_send.at[j], part_in.at[j], p_s.at[j], p_r.at[j], partner)
+        return carry
+
+    def ours(j, carry):
+        cols = pl.ds(pl.multiple_of(j * CHUNK, CHUNK), CHUNK)
+        own_part[:, cols] = jnp.dot(attn[...], w_own[1, :, cols], preferred_element_type=F32)
+        return carry
+
+    def joined(j, carry):
+        got(part_in.at[j], p_s.at[j], p_r.at[j])
+        cols = pl.ds(pl.multiple_of(j * CHUNK, CHUNK), CHUNK)
         out_ref[:, cols] = (own_part[:, cols] + part_in[j].astype(F32)).astype(BF16)
+        return carry
+
+    lax.fori_loop(0, NCH, theirs, 0)
+    lax.fori_loop(0, NCH, ours, 0)
+    lax.fori_loop(0, NCH, joined, 0)
 
     for x_ in xs:
         for n in range(2):
@@ -314,14 +325,12 @@
             for part in range(4):
                 sent(part_ref(z, part, half), c_s.at[n, side, part], c_r.at[n, side, part])
             sent(part_ref(z, 0, half), y_s.at[n, side], y_r.at[n, side])
-    for way in range(2):
-        for i in range(NCH // 2):
-            sent(relay.at[way, i], p_s.at[way, i], p_r.at[way, i])
-            sent(relay.at[way, i], f_s.at[way, i], f_r.at[way, i])
+    for j in range(NCH):
+        sent(part_send.at[j], p_s.at[j], p_r.at[j])
 
 
 def local(queries, keys, values, doc_start, out_weight):
-    docs = jnp.broadcast_to(doc_start[:, None], (doc_start.shape[0], HEAD))
+    docs = doc_start.reshape(1, doc_start.shape[0])
     dma = pltpu.SemaphoreType.DMA
     anyspace = pl.BlockSpec(memory_space=pl.ANY)
     return pl.pallas_call(
@@ -332,7 +341,7 @@
         scratch_shapes=[
             pltpu.VMEM((NZ, NX, NY, NC, 2, STRIPE, HEAD), BF16),
             pltpu.VMEM((NX, STRIPE, GROUP * HEAD), BF16),
-            pltpu.VMEM((NX, STRIPE, HEAD), jnp.int32),
+            pltpu.VMEM((NX, 1, HEAD), jnp.int32),
             pltpu.VMEM((NX, ROWS, HEAD), BF16),
             pltpu.VMEM((NX, ROWS, HEAD), jnp.int32),
             pltpu.VMEM((NX, ROWS, HEAD), F32),
@@ -342,14 +351,13 @@
             pltpu.VMEM((2 * STRIPE, 2 * GROUP * HEAD), BF16),
             pltpu.VMEM((2, 2 * GROUP * HEAD, COLS), BF16),
             pltpu.VMEM((NCH, 2 * STRIPE, CHUNK), BF16),
-            pltpu.VMEM((2, NCH // 2, 2 * STRIPE, CHUNK), BF16),
             pltpu.VMEM((NCH, 2 * STRIPE, CHUNK), BF16),
             pltpu.VMEM((2 * STRIPE, COLS), F32),
             dma((4,)), dma((2,)),
             dma((NX, 2)), dma((NX, 2)), dma((NX,)), dma((NX,)), dma((NX,)), dma((NX,)),
             dma((2, 4, 3)), dma((2, 4, 3)), dma((4,)), dma((4,)), dma((4, 2, 4)), dma((4, 2, 4)),
             dma((2,)), dma((2,)), dma((4, 2)), dma((4, 2)), dma((NX,)), dma((NX,)),
-            dma((2, NCH // 2)), dma((2, NCH // 2)), dma((2, NCH // 2)), dma((2, NCH // 2)),
+            dma((NCH,)), dma((NCH,)),
         ],
         compiler_params=pltpu.CompilerParams(
             collective_id=0, has_side_effects=True, vmem_limit_bytes=56 * 1024 * 1024),

time: 72.2 us -> 64.6 us (0.89)
  Pallas kernels: 67.6 us -> 61.6 us
  local copies, waits for them, and re-layouts: 3.25 us -> 1.88 us
    pallas_call x1, Pallas kernels: 67.6 us -> 61.6 us  [local(): pl.pallas_call(kernel, out_shape=jax.ShapeDtypeStruct((2 * STRIPE, COLS),...]
    broadcast_in_dim x1 -> x0, local copies, waits for them, and re-layouts: 1.37 us -> none  [local(): docs = jnp.broadcast_to(doc_start[:, None], (doc_start.shape[0], HEAD))]
where the time goes in v2:
time: 64.6 us; the launch traced here: 63.5 us
  Pallas kernels  61.6 us (95%)
  local copies, waits for them, and re-layouts  1.88 us (3%)
    pallas_call x1, Pallas kernels, local(): pl.pallas_call(kernel, out_shape=jax.ShapeDtypeStruct((2 * STRIPE, COLS),...  61.6 us
    unnamed x1, local copies, waits for them, and re-layouts  1.88 us

profile of v2, /device:TPU:225, one launch (start us, length us, event | category | flops | bytes accessed | tf_op | source)
XLA Modules:
  0.0 63.5 jit_solution(1095514395170658553)
XLA Ops:
  0.0 61.6 %shard_map.55 = bf16[128,2048]{1,0:T(8,128)(2,1)} custom-call(bf16[128,1024]{1,0:T(8,128)(2,1)} %q_hbm.1, bf16[128,256]{1,0:T(8,128)(2,1)} %k_hbm.1, bf16[128,256]{1,0:T(8,128)(2,1)} %v_hbm.1, s32[1,128]{1,0:T(1,128)} %bitcast.1, bf16[1024,4096]{1,0:T(8,128)(2,1)} %w_hbm.1), custom_call_target="tpu_custom_call" | custom-call | tf_op jit(solution)/shard_map/pallas_call | solution.py:336
  61.6 1.9 %copy.7 = bf16[128,2048]{1,0:T(8,128)(2,1)} copy(bf16[128,2048]{1,0:T(8,128)(2,1)} %shard_map.55) | data formatting | bytes 1048576

commit v3 on v2

--- a/solution.py
+++ b/solution.py
@@ -18,6 +18,9 @@
 COLS = 2048
 CHUNK = 256
 NCH = COLS // CHUNK
+NPIECE = 4
+WROWS = 2 * GROUP * HEAD // (NX * NC * NPIECE)
+WLAG = 18
 MASKED = -1e30
 LOG2 = math.log2(math.e) / math.sqrt(HEAD)
 MESH = pl.DeviceIdType.MESH
@@ -26,10 +29,10 @@
 
 
 def kernel(q_hbm, k_hbm, v_hbm, doc_hbm, w_hbm, out_ref,
-           kv, q_in, doc_in, q_rows, doc_rows, top, acc, attn_send, attn_in, attn, w_own, part_send,
-           part_in, own_part,
-           loc_sem, w_sem, kx_s, kx_r, qx_s, qx_r, dx_s, dx_r, z_s, z_r, c0_s, c0_r, c_s, c_r, y0_s, y0_r,
-           y_s, y_r, o_s, o_r, p_s, p_r):
+           kv, q_in, doc_in, q_rows, doc_rows, top, acc, attn_send, attn_in, attn_far, w_own, w_far,
+           own_part,
+           loc_sem, w_sem, kx_s, kx_r, qx_s, qx_r, dx_s, dx_r, z_s, z_r, c0_s, c0_r, c_s, c_r,
+           y_s, y_r, o_s, o_r, of_s, of_r, wo_s, wo_r, wx_s, wx_r, wy_s, wy_r, wt_s, wt_r):
     c = lax.axis_index("ctx")
     h = lax.axis_index("head")
     z, x, y, core = c // 16, (c // 4) % NX, (c // 2) % NY, c % NC
@@ -42,7 +45,8 @@
     down = dev((z + NZ - 1) % NZ, x, y, core, h)
     across = dev(z, x, 1 - y, core, h)
     twin = dev(z, x, y, 1 - core, h)
-    partner = dev(z, x, y, core, 1 - h)
+    outer = dev(z, x, 1 - y, core, 1 - h)
+    right, left = (x + 1) % NX, (x + NX - 1) % NX
     xs = [(x + d) % NX for d in (2, 1, 3)]
 
     def send(src, dst, ss, rs, to):
@@ -56,7 +60,9 @@
         pltpu.make_async_remote_copy(ref, ref, ss, rs, device_id=twin, device_id_type=MESH).wait_send()
 
     barrier = pltpu.get_barrier_semaphore()
-    peers = [up, down, across, twin, partner] + [dev(z, x_, y, core, h) for x_ in xs]
+    peers = [up, down, across, twin, outer] + [dev(z, x_, y, core, h) for x_ in xs]
+    peers += [dev(z, x_, 1 - y, core, h) for x_ in xs]
+    peers += [dev(z, x_, y, core, 1 - h) for x_ in range(NX)]
     for peer in peers:
         pl.semaphore_signal(barrier, inc=1, device_id=peer, device_id_type=MESH)
 
@@ -78,19 +84,53 @@
         cp.start()
     pl.semaphore_wait(barrier, len(peers))
 
-    for x_ in xs:
-        to = dev(z, x_, y, core, h)
-        send(kv_src(k_hbm, x_), kv.at[z, x, y, core, 0], kx_s.at[x_, 0], kx_r.at[x, 0], to)
-        send(kv_src(v_hbm, x_), kv.at[z, x, y, core, 1], kx_s.at[x_, 1], kx_r.at[x, 1], to)
+    for y_, d_ in ((y, 0), (1 - y, 1)):
+        for x_ in (xs if d_ == 0 else xs + [x]):
+            for n, ref in enumerate((k_hbm, v_hbm)):
+                send(kv_src(ref, x_), kv.at[z, x, y, core, n], kx_s.at[d_, x_, n], kx_r.at[d_, x, n],
+                     dev(z, x_, y_, core, h))
     for x_ in xs:
         to = dev(z, x_, y, core, h)
         send(q_src(x_), q_in.at[x], qx_s.at[x_], qx_r.at[x], to)
         send(doc_hbm, doc_in.at[x], dx_s.at[x_], dx_r.at[x], to)
 
-    w_copies = [
-        pltpu.make_async_copy(w_hbm.at[:, pl.ds(pl.multiple_of((1 - h) * COLS, COLS), COLS)], w_own.at[0], w_sem.at[0]),
-        pltpu.make_async_copy(w_hbm.at[:, pl.ds(pl.multiple_of(h * COLS, COLS), COLS)], w_own.at[1], w_sem.at[1]),
-    ]
+    def w_rows(x_, k_, i_):
+        return pl.ds(pl.multiple_of((x_ * NC + k_) * NPIECE * WROWS + i_ * WROWS, WROWS), WROWS)
+
+    def w_piece(x_, k_, i_):
+        return w_far.at[w_rows(x_, k_, i_)]
+
+    for i in range(NPIECE):
+        send(w_hbm.at[w_rows(x, core, i), pl.ds(pl.multiple_of((1 - h) * COLS, COLS), COLS)],
+             w_piece(x, core, i), wo_s.at[i], wo_r.at[i], outer)
+
+    def w_first(i):
+        ref = w_piece(x, core, i)
+        got(ref, wo_s.at[i], wo_r.at[i])
+        send(ref, ref, wx_s.at[0, i], wx_r.at[0, i], dev(z, right, y, core, h))
+        send(ref, ref, wx_s.at[1, i], wx_r.at[1, i], dev(z, left, y, core, h))
+        send(ref, ref, wt_s.at[0, i], wt_r.at[0, i], twin)
+
+    def w_second(i):
+        for side, (src, dst) in enumerate(((left, right), (right, left))):
+            ref = w_piece(src, core, i)
+            got(ref, wx_s.at[side, i], wx_r.at[side, i])
+
+            @pl.when(i // (NPIECE // 2) == side)
+            def _():
+                n = i % (NPIECE // 2)
+                send(ref, ref, wy_s.at[side, n], wy_r.at[side, n], dev(z, dst, y, core, h))
+
+            send(ref, ref, wt_s.at[1 + side, i], wt_r.at[1 + side, i], twin)
+
+    def w_third(n):
+        for side in range(2):
+            i = side * (NPIECE // 2) + n
+            ref = w_piece((x + 2) % NX, core, i)
+            got(ref, wy_s.at[side, n], wy_r.at[side, n])
+            send(ref, ref, wt_s.at[3, i], wt_r.at[3, i], twin)
+
+    w_copy = pltpu.make_async_copy(w_hbm.at[:, pl.ds(pl.multiple_of(h * COLS, COLS), COLS)], w_own, w_sem.at[0])
 
     def part_ref(zp, part, half=None):
         xb = 2 * (((part + 1) // 2 + 1) % 2)
@@ -99,27 +139,30 @@
             return kv.at[zp, pl.ds(xb, 2), yy, core]
         return kv.at[zp, pl.ds(xb + half, 1), yy, core]
 
+    def own_part_in(part):
+        d_ = part // 2
+        for half in range(2):
+            x_ = 2 * (((part + 1) // 2 + 1) % 2) + half
+
+            def arrive():
+                for n in range(2):
+                    got(kv.at[z, x_, (y + d_) % 2, core, n], kx_s.at[d_, x_, n], kx_r.at[d_, x_, n])
+
+            if d_:
+                arrive()
+            else:
+                pl.when(x_ != x)(arrive)
+
     own_copies[0].wait()
     own_copies[1].wait()
-    for x_ in xs:
-        got(kv.at[z, x_, y, core, 0], kx_s.at[x_, 0], kx_r.at[x_, 0])
-        got(kv.at[z, x_, y, core, 1], kx_s.at[x_, 1], kx_r.at[x_, 1])
-    for part in (1, 0):
+    for part in (0, 1, 2, 3):
+        own_part_in(part)
         ref = part_ref(z, part)
-        send(ref, ref, y0_s.at[part], y0_r.at[part], across)
-        send(ref, ref, z_s.at[0, 0, part], z_r.at[0, 0, part], up)
-        send(ref, ref, z_s.at[1, 0, part], z_r.at[1, 0, part], down)
+        if part < 3:
+            send(ref, ref, z_s.at[0, 0, part], z_r.at[0, 0, part], up)
+            send(ref, ref, z_s.at[1, 0, part], z_r.at[1, 0, part], down)
         send(ref, ref, c0_s.at[part], c0_r.at[part], twin)
-    for cp in w_copies:
-        cp.start()
-    ref = part_ref(z, 2)
-    got(ref, y0_s.at[1], y0_r.at[1])
-    send(ref, ref, z_s.at[0, 0, 2], z_r.at[0, 0, 2], up)
-    send(ref, ref, z_s.at[1, 0, 2], z_r.at[1, 0, 2], down)
-    send(ref, ref, c0_s.at[2], c0_r.at[2], twin)
-    ref = part_ref(z, 3)
-    got(ref, y0_s.at[0], y0_r.at[0])
-    send(ref, ref, c0_s.at[3], c0_r.at[3], twin)
+    w_copy.start()
 
     def twin_ref(zp, part, half=None):
         xb = 2 * (((part + 1) // 2 + 1) % 2)
@@ -253,6 +296,15 @@
                 got(twin_ref(back, part_), c_s.at[s - 2, cs, part_], c_r.at[s - 2, cs, part_])
 
         chunk(s - 1, cs, rb)
+
+        @pl.when((t % 2 == 1) & (t < 2 * NPIECE))
+        def _():
+            w_first(t // 2)
+
+        @pl.when((t % 2 == 0) & (t >= WLAG) & (t < WLAG + 2 * NPIECE))
+        def _():
+            w_second((t - WLAG) // 2)
+
         return carry
 
     lax.fori_loop(0, 32, event, 0)
@@ -261,6 +313,10 @@
     for side in range(2):
         for part in range(4):
             got(twin_ref(far, part, side), c_s.at[3, side, part], c_r.at[3, side, part])
+
+    def place(ref, x_):
+        return ref.at[pl.ds(pl.multiple_of(x_ // 2 * STRIPE, STRIPE), STRIPE),
+                      pl.ds(pl.multiple_of(x_ % 2 * GROUP * HEAD, HEAD), GROUP * HEAD)]
 
     def last(rb, carry):
         chunk(4, 0, rb)
@@ -269,52 +325,44 @@
         for g in range(GROUP):
             attn_send[rb, :, g * HEAD:(g + 1) * HEAD] = o[g * STRIPE:(g + 1) * STRIPE]
 
+        send(attn_send.at[rb], place(attn_far, x), of_s.at[rb], of_r.at[x], dev(z, rb, y, core, 1 - h))
+
         @pl.when(rb != x)
         def _():
-            send(attn_send.at[rb], attn_in.at[x], o_s.at[rb], o_r.at[x], dev(z, rb, y, core, h))
+            send(attn_send.at[rb], place(attn_in, x), o_s.at[rb], o_r.at[x], dev(z, rb, y, core, h))
 
         return carry
 
     lax.fori_loop(0, NX, last, 0)
-    attn_in[x] = attn_send[x]
-
-    for cp in w_copies:
-        cp.wait()
+    home = pltpu.make_async_copy(attn_send.at[x], place(attn_in, x), loc_sem.at[0])
+    home.start()
+
+    for n in range(NPIECE // 2):
+        w_third(n)
+
+    def near(j, carry):
+        cols = pl.ds(pl.multiple_of(j * CHUNK, CHUNK), CHUNK)
+        own_part[:, cols] = jnp.dot(attn_in[...], w_own[:, cols], preferred_element_type=F32)
+        return carry
+
+    def far_too(j, carry):
+        cols = pl.ds(pl.multiple_of(j * CHUNK, CHUNK), CHUNK)
+        rest = jnp.dot(attn_far[...], w_far[:, cols], preferred_element_type=F32)
+        out_ref[:, cols] = (own_part[:, cols] + rest).astype(BF16)
+        return carry
+
+    w_copy.wait()
+    home.wait()
     for x_ in xs:
-        got(attn_in.at[x_], o_s.at[x_], o_r.at[x_])
-    for kind in range(NX):
-        attn[kind // 2 * STRIPE:(kind // 2 + 1) * STRIPE,
-             kind % 2 * GROUP * HEAD:(kind % 2 + 1) * GROUP * HEAD] = attn_in[kind]
-
-    def theirs(j, carry):
-        cols = pl.ds(pl.multiple_of(j * CHUNK, CHUNK), CHUNK)
-        part_send[j] = jnp.dot(attn[...], w_own[0, :, cols], preferred_element_type=F32).astype(BF16)
-        send(part_send.at[j], part_in.at[j], p_s.at[j], p_r.at[j], partner)
-        return carry
-
-    def ours(j, carry):
-        cols = pl.ds(pl.multiple_of(j * CHUNK, CHUNK), CHUNK)
-        own_part[:, cols] = jnp.dot(attn[...], w_own[1, :, cols], preferred_element_type=F32)
-        return carry
-
-    def joined(j, carry):
-        got(part_in.at[j], p_s.at[j], p_r.at[j])
-        cols = pl.ds(pl.multiple_of(j * CHUNK, CHUNK), CHUNK)
-        out_ref[:, cols] = (own_part[:, cols] + part_in[j].astype(F32)).astype(BF16)
-        return carry
-
-    lax.fori_loop(0, NCH, theirs, 0)
-    lax.fori_loop(0, NCH, ours, 0)
-    lax.fori_loop(0, NCH, joined, 0)
-
+        got(place(attn_in, x_), o_s.at[x_], o_r.at[x_])
+    lax.fori_loop(0, NCH, near, 0)
     for x_ in xs:
         for n in range(2):
-            sent(kv.at[z, x_, y, core, n], kx_s.at[x_, n], kx_r.at[x_, n])
+            for d_ in range(2):
+                sent(kv.at[z, x_, y, core, n], kx_s.at[d_, x_, n], kx_r.at[d_, x_, n])
         sent(q_in.at[x_], qx_s.at[x_], qx_r.at[x_])
         sent(doc_in.at[x_], dx_s.at[x_], dx_r.at[x_])
         sent(attn_send.at[x_], o_s.at[x_], o_r.at[x_])
-    for part in range(2):
-        sent(part_ref(z, part), y0_s.at[part], y0_r.at[part])
     for part in range(4):
         sent(part_ref(z, part), c0_s.at[part], c0_r.at[part])
     for n in range(4):
@@ -325,8 +373,27 @@
             for part in range(4):
                 sent(part_ref(z, part, half), c_s.at[n, side, part], c_r.at[n, side, part])
             sent(part_ref(z, 0, half), y_s.at[n, side], y_r.at[n, side])
-    for j in range(NCH):
-        sent(part_send.at[j], p_s.at[j], p_r.at[j])
+    for x_ in range(NX):
+        sent(attn_send.at[x_], of_s.at[x_], of_r.at[x_])
+    for i in range(NPIECE):
+        ref = w_piece(x, core, i)
+        sent(ref, wo_s.at[i], wo_r.at[i])
+        for side in range(2):
+            sent(ref, wx_s.at[side, i], wx_r.at[side, i])
+        for hop in range(4):
+            sent(ref, wt_s.at[hop, i], wt_r.at[hop, i])
+    for n in range(NPIECE // 2):
+        for side in range(2):
+            sent(w_piece(x, core, n), wy_s.at[side, n], wy_r.at[side, n])
+    for n in range(2):
+        sent(kv.at[z, x, y, core, n], kx_s.at[1, x, n], kx_r.at[1, x, n])
+
+    for hop, x_ in enumerate((x, left, right, (x + 2) % NX)):
+        for i in range(NPIECE):
+            got(w_piece(x_, 1 - core, i), wt_s.at[hop, i], wt_r.at[hop, i])
+    for x_ in range(NX):
+        got(place(attn_far, x_), of_s.at[x_], of_r.at[x_])
+    lax.fori_loop(0, NCH, far_too, 0)
 
 
 def local(queries, keys, values, doc_start, out_weight):
@@ -347,17 +414,17 @@
             pltpu.VMEM((NX, ROWS, HEAD), F32),
             pltpu.VMEM((NX, ROWS, 2 * HEAD), F32),
             pltpu.VMEM((NX, STRIPE, GROUP * HEAD), BF16),
-            pltpu.VMEM((NX, STRIPE, GROUP * HEAD), BF16),
             pltpu.VMEM((2 * STRIPE, 2 * GROUP * HEAD), BF16),
-            pltpu.VMEM((2, 2 * GROUP * HEAD, COLS), BF16),
-            pltpu.VMEM((NCH, 2 * STRIPE, CHUNK), BF16),
-            pltpu.VMEM((NCH, 2 * STRIPE, CHUNK), BF16),
+            pltpu.VMEM((2 * STRIPE, 2 * GROUP * HEAD), BF16),
+            pltpu.VMEM((2 * GROUP * HEAD, COLS), BF16),
+            pltpu.VMEM((2 * GROUP * HEAD, COLS), BF16),
             pltpu.VMEM((2 * STRIPE, COLS), F32),
-            dma((4,)), dma((2,)),
-            dma((NX, 2)), dma((NX, 2)), dma((NX,)), dma((NX,)), dma((NX,)), dma((NX,)),
+            dma((4,)), dma((1,)),
+            dma((2, NX, 2)), dma((2, NX, 2)), dma((NX,)), dma((NX,)), dma((NX,)), dma((NX,)),
             dma((2, 4, 3)), dma((2, 4, 3)), dma((4,)), dma((4,)), dma((4, 2, 4)), dma((4, 2, 4)),
-            dma((2,)), dma((2,)), dma((4, 2)), dma((4, 2)), dma((NX,)), dma((NX,)),
-            dma((NCH,)), dma((NCH,)),
+            dma((4, 2)), dma((4, 2)), dma((NX,)), dma((NX,)),
+            dma((NX,)), dma((NX,)), dma((NPIECE,)), dma((NPIECE,)), dma((2, NPIECE)), dma((2, NPIECE)),
+            dma((2, NPIECE // 2)), dma((2, NPIECE // 2)), dma((4, NPIECE)), dma((4, NPIECE)),
         ],
         compiler_params=pltpu.CompilerParams(
             collective_id=0, has_side_effects=True, vmem_limit_bytes=56 * 1024 * 1024),

time: 64.6 us -> 58.5 us (0.906)
  Pallas kernels: 61.6 us -> 55.7 us
    pallas_call x1, Pallas kernels: 61.6 us -> 55.7 us  [local(): pl.pallas_call(kernel, out_shape=jax.ShapeDtypeStruct((2 * STRIPE, COLS),...]
where the time goes in v3:
time: 58.5 us; the launch traced here: 57.6 us
  Pallas kernels  55.7 us (95%)
  local copies, waits for them, and re-layouts  1.88 us (3%)
    pallas_call x1, Pallas kernels, local(): pl.pallas_call(kernel, out_shape=jax.ShapeDtypeStruct((2 * STRIPE, COLS),...  55.7 us
    unnamed x1, local copies, waits for them, and re-layouts  1.88 us

profile of v3, /device:TPU:225, one launch (start us, length us, event | category | flops | bytes accessed | tf_op | source)
XLA Modules:
  0.0 57.6 jit_solution(12512508870604355388)
XLA Ops:
  0.0 55.7 %shard_map.55 = bf16[128,2048]{1,0:T(8,128)(2,1)} custom-call(bf16[128,1024]{1,0:T(8,128)(2,1)} %q_hbm.1, bf16[128,256]{1,0:T(8,128)(2,1)} %k_hbm.1, bf16[128,256]{1,0:T(8,128)(2,1)} %v_hbm.1, s32[1,128]{1,0:T(1,128)} %bitcast.1, bf16[1024,4096]{1,0:T(8,128)(2,1)} %w_hbm.1), custom_call_target="tpu_custom_call" | custom-call | tf_op jit(solution)/shard_map/pallas_call | solution.py:403
  55.7 1.9 %copy.7 = bf16[128,2048]{1,0:T(8,128)(2,1)} copy(bf16[128,2048]{1,0:T(8,128)(2,1)} %shard_map.55) | data formatting | bytes 1048576

commit v4 on v3

--- a/solution.py
+++ b/solution.py
@@ -20,7 +20,8 @@
 NCH = COLS // CHUNK
 NPIECE = 4
 WROWS = 2 * GROUP * HEAD // (NX * NC * NPIECE)
-WLAG = 18
+WLAG = 19
+PAIR = 2
 MASKED = -1e30
 LOG2 = math.log2(math.e) / math.sqrt(HEAD)
 MESH = pl.DeviceIdType.MESH
@@ -171,24 +172,25 @@
             return kv.at[zp, pl.ds(xb, 2), yy, 1 - core]
         return kv.at[zp, pl.ds(xb + half, 1), yy, 1 - core]
 
-    def work(plane, rb, own, docs):
-        def scores(b):
+    def work(plane, base, tiles, own, docs):
+        def scores(r, b):
             keys = kv[plane, b, :, :, 0].reshape(BLOCK, HEAD)
-            s = lax.dot_general(q_rows[rb], keys, (((1,), (1,)), ((), ())), preferred_element_type=F32)
+            s = lax.dot_general(q_rows[base + r], keys, (((1,), (1,)), ((), ())), preferred_element_type=F32)
             if docs:
                 kpos = rnd * ROUND + plane * PLANE + b * BLOCK + lax.broadcasted_iota(jnp.int32, (ROWS, BLOCK), 1)
-                seen = kpos >= jnp.tile(doc_rows[rb], (1, BLOCK // HEAD))
+                seen = kpos >= jnp.tile(doc_rows[base + r], (1, BLOCK // HEAD))
                 if own:
-                    first = rnd * ROUND + (z * 16 + rb * 4 + y * 2 + core) * STRIPE
+                    first = rnd * ROUND + (z * 16 + (base + r) * 4 + y * 2 + core) * STRIPE
                     qpos = first + lax.broadcasted_iota(jnp.int32, (ROWS, BLOCK), 0) % STRIPE
                     seen = seen & (kpos <= qpos)
                 s = jnp.where(seen, s, MASKED)
             return s
 
-        old, total = top[rb], acc[rb]
-        s = scores(0)
-        for b in range(NX):
-            ahead = scores(b + 1) if b + 1 < NX else None
+        s = scores(*tiles[0])
+        for n, (r, b) in enumerate(tiles):
+            ahead = scores(*tiles[n + 1]) if n + 1 < len(tiles) else None
+            if b == 0:
+                old, total = top[base + r], acc[base + r]
             new = jnp.maximum(old, jnp.max(s, axis=1, keepdims=True))
             p = jnp.exp2(s * LOG2 - jnp.tile(new * LOG2, (1, BLOCK // HEAD))).astype(BF16)
             shrink = jnp.exp2((old - new) * LOG2)
@@ -196,24 +198,27 @@
             both = jnp.concatenate([values, jnp.ones((BLOCK, HEAD), BF16)], axis=1)
             total = total * jnp.tile(shrink, (1, 2)) + jnp.dot(p, both, preferred_element_type=F32)
             old, s = new, ahead
-        acc[rb] = total
-        top[rb] = old
-
-    def chunk(d, side, rb):
+            if n + 1 == len(tiles) or tiles[n + 1][0] != r:
+                acc[base + r] = total
+                top[base + r] = old
+
+    every = [(r, b) for r in range(PAIR) for b in range(NX)]
+
+    def chunk(d, side, pair):
         plane = (z + NZ - d + 2 * d * side) % NZ
         earlier = (d > 0) & (plane < z)
-
-        @pl.when((d == 0) & (side == 0))
-        def _():
-            work(z, rb, True, True)
+        for n in range(NX // PAIR):
+            @pl.when((d == 0) & (side == 0) & (pair == n))
+            def _():
+                work(z, n * PAIR, [(r, b) for r, b in every if b <= n * PAIR + r], True, True)
 
         @pl.when(earlier & (rnd == 1))
         def _():
-            work(plane, rb, False, True)
+            work(plane, pair * PAIR, every, False, True)
 
         @pl.when(earlier & (rnd == 0))
         def _():
-            work(plane, rb, False, False)
+            work(plane, pair * PAIR, every, False, False)
 
     def event(t, carry):
         s = t // 8 + 1
@@ -287,21 +292,23 @@
             top[...] = jnp.full(top.shape, MASKED, F32)
             acc[...] = jnp.zeros(acc.shape, F32)
 
-        cs, rb = e // 4, e % 4
-
-        @pl.when((s > 1) & (rb == 0))
-        def _():
-            back = (z + NZ - (s - 1) + 2 * (s - 1) * cs) % NZ
-            for part_ in range(4):
-                got(twin_ref(back, part_), c_s.at[s - 2, cs, part_], c_r.at[s - 2, cs, part_])
-
-        chunk(s - 1, cs, rb)
+        @pl.when(e % 2 == 0)
+        def _():
+            cs, pair = e // 4, (e // 2) % 2
+
+            @pl.when((s > 1) & (pair == 0))
+            def _():
+                back = (z + NZ - (s - 1) + 2 * (s - 1) * cs) % NZ
+                for part_ in range(4):
+                    got(twin_ref(back, part_), c_s.at[s - 2, cs, part_], c_r.at[s - 2, cs, part_])
+
+            chunk(s - 1, cs, pair)
 
         @pl.when((t % 2 == 1) & (t < 2 * NPIECE))
         def _():
             w_first(t // 2)
 
-        @pl.when((t % 2 == 0) & (t >= WLAG) & (t < WLAG + 2 * NPIECE))
+        @pl.when((t % 2 == 1) & (t >= WLAG) & (t < WLAG + 2 * NPIECE))
         def _():
             w_second((t - WLAG) // 2)
 
@@ -318,22 +325,26 @@
         return ref.at[pl.ds(pl.multiple_of(x_ // 2 * STRIPE, STRIPE), STRIPE),
                       pl.ds(pl.multiple_of(x_ % 2 * GROUP * HEAD, HEAD), GROUP * HEAD)]
 
-    def last(rb, carry):
-        chunk(4, 0, rb)
-        total = acc[rb]
-        o = (total[:, :HEAD] / total[:, HEAD:]).astype(BF16)
-        for g in range(GROUP):
-            attn_send[rb, :, g * HEAD:(g + 1) * HEAD] = o[g * STRIPE:(g + 1) * STRIPE]
-
-        send(attn_send.at[rb], place(attn_far, x), of_s.at[rb], of_r.at[x], dev(z, rb, y, core, 1 - h))
-
-        @pl.when(rb != x)
-        def _():
-            send(attn_send.at[rb], place(attn_in, x), o_s.at[rb], o_r.at[x], dev(z, rb, y, core, h))
-
-        return carry
-
-    lax.fori_loop(0, NX, last, 0)
+    def last(pair, carry):
+        chunk(4, 0, pair)
+
+        def finish(r, inner):
+            rb = pair * PAIR + r
+            total = acc[rb]
+            o = (total[:, :HEAD] / total[:, HEAD:]).astype(BF16)
+            for g in range(GROUP):
+                attn_send[rb, :, g * HEAD:(g + 1) * HEAD] = o[g * STRIPE:(g + 1) * STRIPE]
+            send(attn_send.at[rb], place(attn_far, x), of_s.at[rb], of_r.at[x], dev(z, rb, y, core, 1 - h))
+
+            @pl.when(rb != x)
+            def _():
+                send(attn_send.at[rb], place(attn_in, x), o_s.at[rb], o_r.at[x], dev(z, rb, y, core, h))
+
+            return inner
+
+        return lax.fori_loop(0, PAIR, finish, carry)
+
+    lax.fori_loop(0, NX // PAIR, last, 0)
     home = pltpu.make_async_copy(attn_send.at[x], place(attn_in, x), loc_sem.at[0])
     home.start()
 

time: 58.5 us -> 56.6 us (0.968); the launches traced: 57.6 us -> 56.5 us
  Pallas kernels: 55.7 us -> 54.6 us
    pallas_call x1, Pallas kernels: 55.7 us -> 54.6 us  [local(): pl.pallas_call(kernel, out_shape=jax.ShapeDtypeStruct((2 * STRIPE, COLS),...]
where the time goes in v4:
time: 56.6 us; the launch traced here: 56.5 us
  Pallas kernels  54.6 us (96%)
  local copies, waits for them, and re-layouts  1.88 us (3%)
    pallas_call x1, Pallas kernels, local(): pl.pallas_call(kernel, out_shape=jax.ShapeDtypeStruct((2 * STRIPE, COLS),...  54.6 us
    unnamed x1, local copies, waits for them, and re-layouts  1.88 us

profile of v4, /device:TPU:225, one launch (start us, length us, event | category | flops | bytes accessed | tf_op | source)
XLA Modules:
  0.0 56.5 jit_solution(13583076547101334984)
XLA Ops:
  0.0 54.6 %shard_map.55 = bf16[128,2048]{1,0:T(8,128)(2,1)} custom-call(bf16[128,1024]{1,0:T(8,128)(2,1)} %q_hbm.1, bf16[128,256]{1,0:T(8,128)(2,1)} %k_hbm.1, bf16[128,256]{1,0:T(8,128)(2,1)} %v_hbm.1, s32[1,128]{1,0:T(1,128)} %bitcast.1, bf16[1024,4096]{1,0:T(8,128)(2,1)} %w_hbm.1), custom_call_target="tpu_custom_call" | custom-call | tf_op jit(solution)/shard_map/pallas_call | solution.py:414
  54.6 1.9 %copy.7 = bf16[128,2048]{1,0:T(8,128)(2,1)} copy(bf16[128,2048]{1,0:T(8,128)(2,1)} %shard_map.55) | data formatting | bytes 1048576

commit v5 on v4

--- a/solution.py
+++ b/solution.py
@@ -16,7 +16,7 @@
 BLOCK = NY * NC * STRIPE
 ROUND = NZ * PLANE
 COLS = 2048
-CHUNK = 256
+CHUNK = 2048
 NCH = COLS // CHUNK
 NPIECE = 4
 WROWS = 2 * GROUP * HEAD // (NX * NC * NPIECE)
@@ -189,7 +189,9 @@
         s = scores(*tiles[0])
         for n, (r, b) in enumerate(tiles):
             ahead = scores(*tiles[n + 1]) if n + 1 < len(tiles) else None
-            if b == 0:
+            if b == 0 and own:
+                old, total = jnp.full((ROWS, HEAD), MASKED, F32), jnp.zeros((ROWS, 2 * HEAD), F32)
+            elif b == 0:
                 old, total = top[base + r], acc[base + r]
             new = jnp.maximum(old, jnp.max(s, axis=1, keepdims=True))
             p = jnp.exp2(s * LOG2 - jnp.tile(new * LOG2, (1, BLOCK // HEAD))).astype(BF16)
@@ -289,8 +291,6 @@
                 for g in range(GROUP):
                     q_rows[rb_, g * STRIPE:(g + 1) * STRIPE] = q_in[rb_, :, g * HEAD:(g + 1) * HEAD]
                     doc_rows[rb_, g * STRIPE:(g + 1) * STRIPE] = line
-            top[...] = jnp.full(top.shape, MASKED, F32)
-            acc[...] = jnp.zeros(acc.shape, F32)
 
         @pl.when(e % 2 == 0)
         def _():

time: 56.6 us -> 53.9 us (0.952)
  Pallas kernels: 54.6 us -> 51.9 us
    pallas_call x1, Pallas kernels: 54.6 us -> 51.9 us  [local(): pl.pallas_call(kernel, out_shape=jax.ShapeDtypeStruct((2 * STRIPE, COLS),...]
where the time goes in v5:
time: 53.9 us; the launch traced here: 53.8 us
  Pallas kernels  51.9 us (96%)
  local copies, waits for them, and re-layouts  1.88 us (3%)
    pallas_call x1, Pallas kernels, local(): pl.pallas_call(kernel, out_shape=jax.ShapeDtypeStruct((2 * STRIPE, COLS),...  51.9 us
    unnamed x1, local copies, waits for them, and re-layouts  1.88 us

profile of v5, /device:TPU:225, one launch (start us, length us, event | category | flops | bytes accessed | tf_op | source)
XLA Modules:
  0.0 53.8 jit_solution(8988881936828022889)
XLA Ops:
  0.0 51.9 %shard_map.55 = bf16[128,2048]{1,0:T(8,128)(2,1)} custom-call(bf16[128,1024]{1,0:T(8,128)(2,1)} %q_hbm.1, bf16[128,256]{1,0:T(8,128)(2,1)} %k_hbm.1, bf16[128,256]{1,0:T(8,128)(2,1)} %v_hbm.1, s32[1,128]{1,0:T(1,128)} %bitcast.1, bf16[1024,4096]{1,0:T(8,128)(2,1)} %w_hbm.1), custom_call_target="tpu_custom_call" | custom-call | tf_op jit(solution)/shard_map/pallas_call | solution.py:414
  51.9 1.9 %copy.7 = bf16[128,2048]{1,0:T(8,128)(2,1)} copy(bf16[128,2048]{1,0:T(8,128)(2,1)} %shard_map.55) | data formatting | bytes 1048576

commit v6 on v5

--- a/solution.py
+++ b/solution.py
@@ -275,7 +275,7 @@
 
             send(r, r, c_s.at[3, side, part], c_r.at[3, side, part], twin)
 
-        @pl.when(t == 0)
+        @pl.when(t == 1)
         def _():
             own_copies[2].wait()
             own_copies[3].wait()
@@ -292,7 +292,7 @@
                     q_rows[rb_, g * STRIPE:(g + 1) * STRIPE] = q_in[rb_, :, g * HEAD:(g + 1) * HEAD]
                     doc_rows[rb_, g * STRIPE:(g + 1) * STRIPE] = line
 
-        @pl.when(e % 2 == 0)
+        @pl.when(e % 2 == 1)
         def _():
             cs, pair = e // 4, (e // 2) % 2
 
@@ -347,6 +347,16 @@
     lax.fori_loop(0, NX // PAIR, last, 0)
     home = pltpu.make_async_copy(attn_send.at[x], place(attn_in, x), loc_sem.at[0])
     home.start()
+    for part in range(4):
+        sent(part_ref(z, part), c0_s.at[part], c0_r.at[part])
+    for n in range(4):
+        for side in range(2):
+            half = side if n == 3 else None
+            for part in range(3):
+                sent(part_ref(z, part, half), z_s.at[side, n, part], z_r.at[side, n, part])
+            for part in range(4):
+                sent(part_ref(z, part, half), c_s.at[n, side, part], c_r.at[n, side, part])
+            sent(part_ref(z, 0, half), y_s.at[n, side], y_r.at[n, side])
 
     for n in range(NPIECE // 2):
         w_third(n)
@@ -374,16 +384,6 @@
         sent(q_in.at[x_], qx_s.at[x_], qx_r.at[x_])
         sent(doc_in.at[x_], dx_s.at[x_], dx_r.at[x_])
         sent(attn_send.at[x_], o_s.at[x_], o_r.at[x_])
-    for part in range(4):
-        sent(part_ref(z, part), c0_s.at[part], c0_r.at[part])
-    for n in range(4):
-        for side in range(2):
-            half = side if n == 3 else None
-            for part in range(3):
-                sent(part_ref(z, part, half), z_s.at[side, n, part], z_r.at[side, n, part])
-            for part in range(4):
-                sent(part_ref(z, part, half), c_s.at[n, side, part], c_r.at[n, side, part])
-            sent(part_ref(z, 0, half), y_s.at[n, side], y_r.at[n, side])
     for x_ in range(NX):
         sent(attn_send.at[x_], of_s.at[x_], of_r.at[x_])
     for i in range(NPIECE):

time: 53.9 us -> 52.3 us (0.970)
  Pallas kernels: 51.9 us -> 50.3 us
    pallas_call x1, Pallas kernels: 51.9 us -> 50.3 us  [local(): pl.pallas_call(kernel, out_shape=jax.ShapeDtypeStruct((2 * STRIPE, COLS),...]
where the time goes in v6:
time: 52.3 us; the launch traced here: 52.2 us
  Pallas kernels  50.3 us (96%)
  local copies, waits for them, and re-layouts  1.88 us (4%)
    pallas_call x1, Pallas kernels, local(): pl.pallas_call(kernel, out_shape=jax.ShapeDtypeStruct((2 * STRIPE, COLS),...  50.3 us
    unnamed x1, local copies, waits for them, and re-layouts  1.88 us

profile of v6, /device:TPU:225, one launch (start us, length us, event | category | flops | bytes accessed | tf_op | source)
XLA Modules:
  0.0 52.2 jit_solution(15204040714530713277)
XLA Ops:
  0.0 50.3 %shard_map.55 = bf16[128,2048]{1,0:T(8,128)(2,1)} custom-call(bf16[128,1024]{1,0:T(8,128)(2,1)} %q_hbm.1, bf16[128,256]{1,0:T(8,128)(2,1)} %k_hbm.1, bf16[128,256]{1,0:T(8,128)(2,1)} %v_hbm.1, s32[1,128]{1,0:T(1,128)} %bitcast.1, bf16[1024,4096]{1,0:T(8,128)(2,1)} %w_hbm.1), custom_call_target="tpu_custom_call" | custom-call | tf_op jit(solution)/shard_map/pallas_call | solution.py:414
  50.3 1.9 %copy.7 = bf16[128,2048]{1,0:T(8,128)(2,1)} copy(bf16[128,2048]{1,0:T(8,128)(2,1)} %shard_map.55) | data formatting | bytes 1048576

commit v7 on v6

--- a/solution.py
+++ b/solution.py
@@ -20,7 +20,7 @@
 NCH = COLS // CHUNK
 NPIECE = 4
 WROWS = 2 * GROUP * HEAD // (NX * NC * NPIECE)
-WLAG = 19
+WLAG = 18
 PAIR = 2
 MASKED = -1e30
 LOG2 = math.log2(math.e) / math.sqrt(HEAD)
@@ -304,11 +304,11 @@
 
             chunk(s - 1, cs, pair)
 
-        @pl.when((t % 2 == 1) & (t < 2 * NPIECE))
+        @pl.when((t % 2 == 0) & (t < 2 * NPIECE))
         def _():
             w_first(t // 2)
 
-        @pl.when((t % 2 == 1) & (t >= WLAG) & (t < WLAG + 2 * NPIECE))
+        @pl.when((t % 2 == 0) & (t >= WLAG) & (t < WLAG + 2 * NPIECE))
         def _():
             w_second((t - WLAG) // 2)
 

time: 52.3 us -> 52.3 us (level)
  no operation moved by 1% of the time
where the time goes in v7:
time: 52.3 us; the launch traced here: 52.2 us
  Pallas kernels  50.3 us (96%)
  local copies, waits for them, and re-layouts  1.88 us (4%)
    pallas_call x1, Pallas kernels, local(): pl.pallas_call(kernel, out_shape=jax.ShapeDtypeStruct((2 * STRIPE, COLS),...  50.3 us
    unnamed x1, local copies, waits for them, and re-layouts  1.88 us

profile of v7, /device:TPU:225, one launch (start us, length us, event | category | flops | bytes accessed | tf_op | source)
XLA Modules:
  0.0 52.2 jit_solution(202479360149217255)
XLA Ops:
  0.0 50.3 %shard_map.55 = bf16[128,2048]{1,0:T(8,128)(2,1)} custom-call(bf16[128,1024]{1,0:T(8,128)(2,1)} %q_hbm.1, bf16[128,256]{1,0:T(8,128)(2,1)} %k_hbm.1, bf16[128,256]{1,0:T(8,128)(2,1)} %v_hbm.1, s32[1,128]{1,0:T(1,128)} %bitcast.1, bf16[1024,4096]{1,0:T(8,128)(2,1)} %w_hbm.1), custom_call_target="tpu_custom_call" | custom-call | tf_op jit(solution)/shard_map/pallas_call | solution.py:414
  50.3 1.9 %copy.7 = bf16[128,2048]{1,0:T(8,128)(2,1)} copy(bf16[128,2048]{1,0:T(8,128)(2,1)} %shard_map.55) | data formatting | bytes 1048576
